TPU v7x, 32 devices: a whole 2x2x4 slice. The times are simulated.
32 devices in a mesh: grp: 4 (over x, core), mem: 8 (over z, y).
Axes of the slice: x: 2, y: 2, z: 4, core: 2. Of those that a mesh axis runs over, the one named last changes fastest.
Arguments:
- features: bfloat16 [32768, 4096], P(('grp', 'mem')), may hold values from -0.09375 to 0.09375
- re_features: bfloat16 [32768, 256], P(('grp', 'mem')), may hold values from -6 to 6
- member_id: int32 [32768], P(('grp', 'mem')), may hold values from 0 to 255, as said below
- slot: int32 [32768], P(('grp', 'mem')), may hold values from 0 to 2047, as said below
- labels: int32 [32768], P(('grp', 'mem')), may hold values 0 or 1
- offsets: float32 [32768], P(('grp', 'mem')), may hold values from -6 to 6
- feature_scale: float32 [4096], replicated, may hold values from 0.3 to 3
- w_start: float32 [4096], replicated, may hold values from -4 to 4
Outputs:
- fixed_weights: float32 [4096], replicated
- member_coef: float32 [256, 256], P(('grp', 'mem'))
- row_offsets: float32 [32768], P(('grp', 'mem'))
Inputs may be any that keep to these rules, and one draw needn't show every extreme that they name: A row of device k (devices counted along grp, then mem) belongs to group k // 8: member_id // 64 is that group, and (member_id mod 64) // 8 equals slot // 256. Rows per member are uneven. Within one device's rows the slots are distinct; slot // 256 is the mem index that owns the row's member, so at most 256 rows of one device go to one owner, and in every group one owner receives exactly 256 rows from every device of the group.
All inputs are finite; a program needn't handle non-finite values. No bound on the sum of `labels` on one device may be relied on, other than what follows from the above.
Results may differ from a plain program's by a relative error of at most 0.0003.
Values may be sent and summed in bfloat16 or wider, within the bound.
A program may use at most 64 MiB of HBM per device.

v0:
```python
import jax
import jax.numpy as jnp
from jax import lax
from jax.sharding import PartitionSpec as P

MEM_DEV = 8
NEWTON = 2
CG_ITERS = 3


ridge_fixed = 1.0
ridge_member = 1.0


def split_pair(values):
    upper_part = values.astype(jnp.bfloat16)
    held_part = lax.optimization_barrier(upper_part)
    lower_part = (values - held_part.astype(jnp.float32)).astype(jnp.bfloat16)
    return (upper_part, lower_part)


def split_two(vector):
    upper_part, lower_part = split_pair(vector)
    return jnp.stack([upper_part, lower_part], axis=1)


def apply_rows(features, vector):
    return jnp.sum(jnp.dot(features, split_two(vector), preferred_element_type=jnp.float32), axis=1)


def apply_columns(features, values):
    pair_cols = split_two(values)
    product = lax.dot_general(
        pair_cols, features, (((0,), (0,)), ((), ())), preferred_element_type=jnp.float32
    )
    return jnp.sum(product, axis=0)


def inner_rows(left, right):
    return lax.dot_general(
        left, right, (((0,), (0,)), ((), ())), preferred_element_type=jnp.float32
    )


def hessian_times(features, feature_scale, curvature, direction):
    inner = curvature * apply_rows(features, feature_scale * direction)
    summed = lax.psum(apply_columns(features, inner), ("grp", "mem"))
    return feature_scale * summed + ridge_fixed * direction


def fit_members(received, arrived):
    curv_row = arrived[0]
    resid_row = arrived[1]
    local_row = arrived[2]
    onehot = (local_row[:, None] == jnp.arange(MEM_DEV).astype(arrived.dtype)[None, :]).astype(
        arrived.dtype
    )
    z_float = received.astype(jnp.float32)

    def gram_one(column):
        upper_part, lower_part = split_pair(z_float * (curv_row * column)[:, None])
        return inner_rows(received, upper_part) + inner_rows(received, lower_part)

    gram_all = lax.map(gram_one, onehot.T) + ridge_member * jnp.eye(
        received.shape[1], dtype=jnp.float32
    )
    grad_upper, grad_lower = split_pair(resid_row[:, None] * onehot)
    member_grad = inner_rows(grad_upper, received) + inner_rows(grad_lower, received)
    factor = jnp.linalg.cholesky(gram_all)
    member_coef = -jax.scipy.linalg.cho_solve((factor, True), member_grad[:, :, None])[:, :, 0]
    coef_upper, coef_lower = split_pair(member_coef)
    scores = jnp.dot(received, coef_upper.T, preferred_element_type=jnp.float32) + jnp.dot(
        received, coef_lower.T, preferred_element_type=jnp.float32
    )
    return (member_coef, jnp.sum(scores * onehot, axis=1))


def on_device(features, re_features, member_id, slot, labels, offsets, feature_scale, w_start):
    row_count = features.shape[0]
    slots_all = 2 * row_count
    packed = jnp.zeros((slots_all, re_features.shape[1]), jnp.bfloat16).at[slot].set(re_features)
    received = None
    target = labels.astype(jnp.float32)
    weights = w_start
    for newton_step in range(NEWTON):
        margin = apply_rows(features, feature_scale * weights) + offsets
        probability = jax.nn.sigmoid(margin)
        curvature = probability * (1.0 - probability)
        summed = lax.psum(apply_columns(features, probability - target), ("grp", "mem"))
        gradient = feature_scale * summed + ridge_fixed * weights
        residual = -gradient
        direction = residual
        res_norm = jnp.sum(residual * residual)
        update = jnp.zeros_like(weights)
        for cg_step in range(CG_ITERS):
            hess_image = hessian_times(features, feature_scale, curvature, direction)
            step_size = res_norm / jnp.sum(direction * hess_image)
            update = update + step_size * direction
            residual = residual - step_size * hess_image
            next_norm = jnp.sum(residual * residual)
            direction = residual + next_norm / res_norm * direction
            res_norm = next_norm
        weights = weights + update
    score = apply_rows(features, feature_scale * weights)
    probability = jax.nn.sigmoid(score)
    curvature = probability * (1.0 - probability)
    resid_row = probability - target
    local_id = (member_id % MEM_DEV).astype(jnp.float32)
    row_weights = jnp.stack([curvature, resid_row, local_id], axis=0)
    weight_slots = jnp.zeros((3, slots_all), jnp.float32).at[:, slot].set(row_weights)
    received = lax.all_to_all(packed, "mem", split_axis=0, concat_axis=0, tiled=True)
    arrived = lax.all_to_all(weight_slots, "mem", split_axis=1, concat_axis=1, tiled=True)
    member_coef, slot_scores = fit_members(received, arrived)
    returned = lax.all_to_all(slot_scores, "mem", split_axis=0, concat_axis=0, tiled=True)
    row_offsets = returned[slot]
    return (weights, member_coef, row_offsets)


def solution(mesh):
    placed = (
        P(("grp", "mem"), None),
        P(("grp", "mem"), None),
        P(("grp", "mem")),
        P(("grp", "mem")),
        P(("grp", "mem")),
        P(("grp", "mem")),
        P(),
        P(),
    )
    return jax.shard_map(
        on_device,
        mesh=mesh,
        in_specs=placed,
        out_specs=(P(), P(("grp", "mem"), None), P(("grp", "mem"))),
        check_vma=False,
    )
```

profile of v0, /device:TPU:0, one launch (start us, length us, event | category | flops | bytes accessed | tf_op | source)
XLA Modules:
  0.0 981.4 jit_solution(12740496581098813807)
XLA Ops:
  1.5 5.8 convolution_reduce_fusion.16
  8.6 42.1 %psum.56 = f32[4096]{0:T(1024)S(1)} all-reduce(f32[4096]{0:T(1024)S(1)} %convolution_reduce_fusion.7), channel_id=1, replica_groups=mesh['grp'=4,'mem'=8] {'grp','mem'}, use_global_device_ids=true, to_apply=%region_2.0 | all-reduce | flops 4096 | bytes 32768 | tf_op jit(solution)/shard_map/psum | solution.py:89
  50.8 5.8 convolution_reduce_fusion.15
  57.9 40.2 %psum.57 = f32[4096]{0:T(1024)S(1)} all-reduce(f32[4096]{0:T(1024)S(1)} %convolution_reduce_fusion.6), channel_id=1, replica_groups=mesh['grp'=4,'mem'=8] {'grp','mem'}, use_global_device_ids=true, to_apply=%region_6.0 | all-reduce | flops 4096 | bytes 32768 | tf_op jit(solution)/shard_map/psum | solution.py:47
  102.1 5.7 convolution_reduce_fusion.14
  112.4 40.2 %psum.58 = f32[4096]{0:T(1024)S(1)} all-reduce(f32[4096]{0:T(1024)S(1)} %convolution_reduce_fusion.5), channel_id=1, replica_groups=mesh['grp'=4,'mem'=8] {'grp','mem'}, use_global_device_ids=true, to_apply=%region_11.0 | all-reduce | flops 4096 | bytes 32768 | tf_op jit(solution)/shard_map/psum | solution.py:47
  166.9 40.2 %psum.59 = f32[4096]{0:T(1024)S(1)} all-reduce(f32[4096]{0:T(1024)S(1)} %convolution_reduce_fusion.4), channel_id=1, replica_groups=mesh['grp'=4,'mem'=8] {'grp','mem'}, use_global_device_ids=true, to_apply=%region_16.0 | all-reduce | flops 4096 | bytes 32768 | tf_op jit(solution)/shard_map/psum | solution.py:47
  219.5 40.1 %psum.60 = f32[4096]{0:T(1024)S(1)} all-reduce(f32[4096]{0:T(1024)S(1)} %convolution_reduce_fusion.3), channel_id=1, replica_groups=mesh['grp'=4,'mem'=8] {'grp','mem'}, use_global_device_ids=true, to_apply=%region_20.0 | all-reduce | flops 4096 | bytes 32768 | tf_op jit(solution)/shard_map/psum | solution.py:89
  269.9 40.7 %psum.61 = f32[4096]{0:T(1024)S(1)} all-reduce(f32[4096]{0:T(1024)S(1)} %convolution_reduce_fusion.2), channel_id=1, replica_groups=mesh['grp'=4,'mem'=8] {'grp','mem'}, use_global_device_ids=true, to_apply=%region_24.0 | all-reduce | flops 4096 | bytes 32768 | tf_op jit(solution)/shard_map/psum | solution.py:47
  314.5 5.7 convolution_reduce_fusion.10
  324.8 39.9 %psum.62 = f32[4096]{0:T(1024)S(1)} all-reduce(f32[4096]{0:T(1024)S(1)} %convolution_reduce_fusion.1), channel_id=1, replica_groups=mesh['grp'=4,'mem'=8] {'grp','mem'}, use_global_device_ids=true, to_apply=%region_29.0 | all-reduce | flops 4096 | bytes 32768 | tf_op jit(solution)/shard_map/psum | solution.py:47
  368.7 5.7 convolution_reduce_fusion.9
  379.1 40.3 %psum.63 = f32[4096]{0:T(1024)S(1)} all-reduce(f32[4096]{0:T(1024)S(1)} %convolution_reduce_fusion), channel_id=1, replica_groups=mesh['grp'=4,'mem'=8] {'grp','mem'}, use_global_device_ids=true, to_apply=%region_34.0 | all-reduce | flops 4096 | bytes 32768 | tf_op jit(solution)/shard_map/psum | solution.py:47
  438.2 6.4 scatter_custom_fusion.1
  444.9 5.7 all-to-all-start.1
  453.3 22.0 %all-to-all-done.1 = bf16[8,256,256]{2,1,0:T(8,128)(2,1)S(1)} async-done(((bf16[8,256,256]{2,1,0:T(8,128)(2,1)}), bf16[8,256,256]{2,1,0:T(8,128)(2,1)S(1)}, u32[]{:S(2)}, u32[]{:S(2)}) %all-to-all-start.1) | async-done | bytes 1048608 | tf_op jit(solution)/shard_map/all_to_all | solution.py:111
  476.4 19.9 %while.11 = (s32[]{:T(128)}, f32[8,256,256]{1,2,0:T(8,128)}, f32[8,2048]{1,0:T(8,128)S(1)}, f32[2048]{0:T(1024)S(1)}, f32[2048,256]{1,0:T(8,128)S(1)}, /*index=5*/bf16[2048,256]{1,0:T(8,128)(2,1)S(1)}, s32[]{:T(128)}) while((s32[]{:T(128)}, f32[8,256,256]{1,2,0:T(8,128)}, f32[8,2048]{1,0:T(8,128)S(1)}, f32[2048]{0:T(1024)S(1)}, ...), condition=%wide.region_40.41_spmd, body=%wide.region_39.40_spmd.sunk | while | flops 540084224 | bytes 10281053 | solution.py:64
  505.7 94.4 %custom-call.20 = f32[8,128,128]{2,1,0:T(8,128)} custom-call(f32[8,128,128]{2,1,0:T(8,128)S(1)} %cholesky.119), custom_call_target="Cholesky" | custom-call | tf_op jit(solution)/shard_map/jit(cholesky)/cholesky | solution.py:69
  602.3 80.0 %custom-call.21 = f32[8,1,128,128]{2,3,1,0:T(8,128)} custom-call(f32[8,1,128,128]{3,2,1,0:T(8,128)} %select_bitcast_fusion), custom_call_target="InvertDiagBlocksLowerTriangular" | custom-call | tf_op jit(solution)/shard_map/jit(cholesky)/cholesky | solution.py:69
  687.3 95.4 %custom-call.22 = f32[8,128,128]{2,1,0:T(8,128)} custom-call(f32[8,128,128]{2,1,0:T(8,128)} %convolution_subtract_fusion), custom_call_target="Cholesky" | custom-call | tf_op jit(solution)/shard_map/jit(cholesky)/cholesky | solution.py:69
  787.8 5.9 while.12
  793.7 158.7 %custom-call.23 = f32[8,2,128,128]{2,3,1,0:T(8,128)} custom-call(f32[8,2,128,128]{3,2,1,0:T(8,128)} %bitcast.163), custom_call_target="InvertDiagBlocksLowerTriangular" | custom-call | tf_op jit(solution)/shard_map/jit(_cho_solve)/vmap()/triangular_solve | solution.py:70
  960.9 9.7 all_to_all.33
  970.6 10.5 %gather_fusion = f32[1024]{0:T(1024)} fusion(f32[2048]{0:T(1024)S(1)} %bitcast.135, s32[1024]{0:T(1024)S(1)} %copy-done.20), kind=kCustom, calls=%fused_computation | custom fusion | bytes 12288 | tf_op jit(solution)/shard_map/gather | solution.py:115
  (238 shorter events, 130.7 us)
Async XLA Ops:
  1.4 5.9 copy-start.12
  1.4 5.9 copy-start.19
  1.4 5.9 copy-start
  7.4 43.3 %copy-start.4 = (f32[4096]{0:T(1024)S(1)}, f32[4096]{0:T(1024)}, u32[]{:S(2)}) copy-start(f32[4096]{0:T(1024)} %param.16) | copy-start | bytes 49156
  7.4 43.3 %copy-start.8 = (f32[4096]{0:T(1024)S(1)}, f32[4096]{0:T(1024)}, u32[]{:S(2)}) copy-start(f32[4096]{0:T(1024)} %param.17) | copy-start | bytes 49156
  50.8 5.9 copy-start.1
  374.5 47.5 %copy-start.23 = (s32[1024]{0:T(1024)S(1)}, s32[1024]{0:T(1024)}, u32[]{:S(2)}) copy-start(s32[1024]{0:T(1024)} %param.13) | copy-start | bytes 12292
  374.5 48.1 %copy-start.24 = (s32[1024]{0:T(1024)S(1)}, s32[1024]{0:T(1024)}, u32[]{:S(2)}) copy-start(s32[1024]{0:T(1024)} %param.12) | copy-start | bytes 12292
  433.0 11.9 %all-to-all-start = ((f32[3,8,256]{2,0,1:T(4,128)}), f32[3,8,256]{2,0,1:T(4,128)S(1)}, u32[]{:S(2)}, u32[]{:S(2)}) async-start(f32[3,8,256]{2,0,1:T(4,128)} %copy.32), calls=%async_computation | async-start | bytes 65536 | tf_op jit(solution)/shard_map/all_to_all | solution.py:112
  444.9 30.4 %all-to-all-start.1 = ((bf16[8,256,256]{2,1,0:T(8,128)(2,1)}), bf16[8,256,256]{2,1,0:T(8,128)(2,1)S(1)}, u32[]{:S(2)}, u32[]{:S(2)}) async-start(bf16[8,256,256]{2,1,0:T(8,128)(2,1)} %bitcast.10), calls=%async_computation.1 | async-start | bytes 2097152 | tf_op jit(solution)/shard_map/all_to_all | solution.py:111
  450.7 24.6 %copy-start.21 = (f32[8]{0:T(128)}, f32[8]{0:T(128)S(1)}, u32[]{:S(2)}) copy-start(f32[8]{0:T(128)S(1)} %iota_convert_fusion) | copy-start | bytes 100
  452.5 22.8 %copy-start.9 = (f32[1,8,256]{2,0,1:T(1,128)}, f32[1,8,256]{2,0,1:T(1,128)S(1)}, u32[]{:S(2)}) copy-start(f32[1,8,256]{2,0,1:T(1,128)S(1)} %get-tuple-element.123) | copy-start | bytes 24580
  505.7 95.8 %copy-start.14 = (pred[128,128]{1,0:T(8,128)(4,1)S(1)}, pred[128,128]{1,0:T(8,128)(4,1)}, u32[]{:S(2)}) copy-start(pred[128,128]{1,0:T(8,128)(4,1)} %iota_compare_fusion.2) | copy-start | bytes 49156
  682.4 100.4 %copy-start.10 = (f32[1,8,256]{2,0,1:T(1,128)S(1)}, f32[1,8,256]{2,0,1:T(1,128)}, u32[]{:S(2)}) copy-start(f32[1,8,256]{2,0,1:T(1,128)} %copy-done.9) | copy-start | bytes 24580
  682.4 100.4 %copy-start.11 = (bf16[2048,8]{0,1:T(8,128)(2,1)S(1)}, bf16[2048,8]{0,1:T(8,128)(2,1)}, u32[]{:S(2)}) copy-start(bf16[2048,8]{0,1:T(8,128)(2,1)} %select_convert_fusion) | copy-start | bytes 98308
  682.4 100.4 %copy-start.15 = (f32[8,256]{1,0:T(8,128)S(1)}, f32[8,256]{1,0:T(8,128)}, u32[]{:S(2)}) copy-start(f32[8,256]{1,0:T(8,128)} %fusion.128) | copy-start | bytes 24580
  682.4 100.4 %copy-start.22 = (f32[8]{0:T(128)S(1)}, f32[8]{0:T(128)}, u32[]{:S(2)}) copy-start(f32[8]{0:T(128)} %copy-done.21) | copy-start | bytes 100
  684.3 98.8 %copy-start.13 = (pred[128,128]{1,0:T(8,128)(4,1)S(1)}, pred[128,128]{1,0:T(8,128)(4,1)}, u32[]{:S(2)}) copy-start(pred[128,128]{1,0:T(8,128)(4,1)} %iota_compare_fusion.3) | copy-start | bytes 49156
  783.1 4.6 copy-start.16
  787.8 164.6 %slice-start = ((f32[8,256,1]{1,0,2:T(8,128)}), f32[8,128,1]{1,0,2:T(8,128)S(1)}, s32[]{:S(2)}) async-start(f32[8,256,1]{1,0,2:T(8,128)} %copy-done.16), calls=%async_computation.3 | async-start | bytes 8192 | tf_op jit(solution)/shard_map/jit(_cho_solve)/vmap()/triangular_solve | solution.py:70
  787.8 167.2 %copy-start.17 = (f32[8,256,1]{1,0,2:T(8,128)S(1)}, f32[8,256,1]{1,0,2:T(8,128)}, u32[]{:S(2)}) copy-start(f32[8,256,1]{1,0,2:T(8,128)} %copy-done.16) | copy-start | bytes 24580
  952.4 6.8 copy-start.7
  956.6 14.0 %copy-start.20 = (s32[1024]{0:T(1024)S(1)}, s32[1024]{0:T(1024)}, u32[]{:S(2)}) copy-start(s32[1024]{0:T(1024)} %get-tuple-element.126) | copy-start | bytes 12292
  960.1 21.1 %copy-start.18 = (f32[8,256]{1,0:T(8,128)}, f32[8,256]{1,0:T(8,128)S(1)}, u32[]{:S(2)}) copy-start(f32[8,256]{1,0:T(8,128)S(1)} %get-tuple-element.95) | copy-start | bytes 24580
  (5 other events, 9.0 us)
where the time goes:
time: 991 us; the launch traced here: 981 us
  other arithmetic  452 us (46%)
  blocking collectives  333 us (34%)
  matrix products  113 us (11%)
  local copies, waits for them, and re-layouts  35 us (4%)
  waiting for transfers between devices  22.3 us (2%)
  between operations  15.2 us (2%)
  starting transfers between devices  10.9 us (1%)
    another operation x9, other arithmetic, fit_members(): factor = jnp.linalg.cholesky(gram_all)  273 us
    psum x6, blocking collectives, hessian_times(): summed = lax.psum(apply_columns(features, inner), ('grp', 'mem'))  241 us
    another operation x6, other arithmetic, fit_members(): jax.scipy.linalg.cho_solve((factor, True), member_grad[:, :, None])[:, :, 0]  161 us
    psum x2, blocking collectives, on_device(): lax.psum(apply_columns(features, probability - target), ('grp', 'mem'))  82.1 us
    dot_general x9, matrix products, apply_rows(): jnp.dot(features, split_two(vector), preferred_element_type=jnp.float32)  51.3 us
    dot_general x8, matrix products, apply_columns(): lax.dot_general(pair_cols, features, (((0,), (0,)), ((), ())), preferred_...  29.9 us
    all_to_all x1, waiting for transfers between devices, on_device(): lax.all_to_all(packed, 'mem', split_axis=0, concat_axis=0, tiled=True)  22 us
  transfers between devices with their start and end apart: 2, of which 2 were waited for; matrix products, arithmetic and copies ran while one was open for 1% of the time, Pallas kernels for 0%

commit v1 on v0

v1 whole, which is shorter than its diff:
```python
import functools

import jax
import jax.numpy as jnp
from jax import lax
from jax.experimental import pallas as pl
from jax.experimental.pallas import tpu as pltpu
from jax.sharding import PartitionSpec as P

MEM_DEV = 8
NEWTON = 2
CG_ITERS = 3
LANES = 128
BLOCK = 32

ridge_fixed = 1.0
ridge_member = 1.0
MESH_ID = pl.DeviceIdType.MESH
NT = (((1,), (1,)), ((), ()))
NN = (((1,), (0,)), ((), ()))
TN = (((0,), (0,)), ((), ()))


def pair_rows(row):
    upper = row.astype(jnp.bfloat16).astype(jnp.float32)
    lower = (row - upper).astype(jnp.bfloat16).astype(jnp.float32)
    at = lax.broadcasted_iota(jnp.int32, (16, row.shape[1]), 0)
    both = jnp.where(at == 0, upper, jnp.where(at == 1, lower, 0.0))
    return both.astype(jnp.bfloat16)


def fit_kernel(
    n_grp, n_mem,
    feat, label_ref, offset_ref, scale_ref, start_ref,
    weight_ref, curv_ref, resid_ref,
    vec_w, vec_u, vec_r, vec_p, curv, send, recv, send_sem, recv_sem,
):
    rows, width = feat.shape
    lines = width // LANES
    me_grp = lax.axis_index("grp")
    me_mem = lax.axis_index("mem")

    partners = []
    for name, me, size in (("mem", me_mem, n_mem), ("grp", me_grp, n_grp)):
        bit = 1
        while bit < size:
            other = me + bit * (1 - 2 * ((me // bit) % 2))
            partners.append(
                (me_grp, other) if name == "mem" else (other, me_mem)
            )
            bit *= 2

    barrier = pltpu.get_barrier_semaphore()
    for partner in partners:
        pl.semaphore_signal(barrier, inc=1, device_id=partner, device_id_type=MESH_ID)
    pl.semaphore_wait(barrier, len(partners))

    def all_sum(value, call):
        for step, partner in enumerate(partners):
            send[call, step] = value
            copy = pltpu.make_async_remote_copy(
                src_ref=send.at[call, step],
                dst_ref=recv.at[call, step],
                send_sem=send_sem.at[call, step],
                recv_sem=recv_sem.at[call, step],
                device_id=partner,
                device_id_type=MESH_ID,
            )
            copy.start()
            copy.wait()
            value = value + recv[call, step]
        return value

    def times_rows(vector):
        row = jnp.concatenate([vector[i : i + 1, :] for i in range(lines)], axis=1)
        pair = pair_rows(row)
        parts = []
        for first in range(0, rows, 256):
            got = lax.dot_general(
                pair, feat[first : first + 256, :], NT, preferred_element_type=jnp.float32
            )
            parts.append(got[0:1] + got[1:2])
        return jnp.concatenate(parts, axis=1)

    def times_columns(row):
        pair = pair_rows(row)
        parts = []
        for first in range(0, width, 256):
            got = lax.dot_general(
                pair, feat[:, first : first + 256], NN, preferred_element_type=jnp.float32
            )
            got = got[0:1] + got[1:2]
            parts += [got[:, at : at + LANES] for at in range(0, 256, LANES)]
        return jnp.concatenate(parts, axis=0)

    def total(value):
        return jnp.sum(jnp.sum(value, axis=1, keepdims=True), axis=0, keepdims=True)

    scale = scale_ref[...]
    target = label_ref[...].astype(jnp.float32)
    vec_w[...] = start_ref[...]

    def newton(step, carry):
        base = step * (CG_ITERS + 1)
        weights = vec_w[...]
        margin = times_rows(scale * weights) + offset_ref[...]
        prob = 1.0 / (1.0 + jnp.exp(-margin))
        curv[...] = prob * (1.0 - prob)
        summed = all_sum(times_columns(prob - target), base)
        resid = -(scale * summed + ridge_fixed * weights)
        vec_r[...] = resid
        vec_p[...] = resid
        vec_u[...] = jnp.zeros_like(resid)

        def cg(k, norm):
            direction = vec_p[...]
            inner = curv[...] * times_rows(scale * direction)
            image = scale * all_sum(times_columns(inner), base + 1 + k) + ridge_fixed * direction
            size = norm / total(direction * image)
            vec_u[...] = vec_u[...] + size * direction
            left = vec_r[...] - size * image
            vec_r[...] = left
            new_norm = total(left * left)
            vec_p[...] = left + new_norm / norm * direction
            return new_norm

        lax.fori_loop(0, CG_ITERS, cg, total(resid * resid))
        vec_w[...] = weights + vec_u[...]
        return carry

    lax.fori_loop(0, NEWTON, newton, 0)
    weights = vec_w[...]
    weight_ref[...] = weights
    score = times_rows(scale * weights)
    prob = 1.0 / (1.0 + jnp.exp(-score))
    curv_ref[...] = prob * (1.0 - prob)
    resid_ref[...] = prob - target


def fit_fixed(features, labels, offsets, feature_scale, w_start, n_grp, n_mem):
    rows, width = features.shape
    lines = width // LANES
    steps = (n_grp.bit_length() - 1) + (n_mem.bit_length() - 1)
    calls = NEWTON * (CG_ITERS + 1)
    line = jax.ShapeDtypeStruct((lines, LANES), jnp.float32)
    row = jax.ShapeDtypeStruct((1, rows), jnp.float32)
    held = pltpu.VMEM((lines, LANES), jnp.float32)
    whole = pl.BlockSpec(memory_space=pltpu.VMEM)
    return pl.pallas_call(
        functools.partial(fit_kernel, n_grp, n_mem),
        out_shape=(line, row, row),
        in_specs=[whole] * 5,
        out_specs=(whole,) * 3,
        scratch_shapes=[
            held, held, held, held,
            pltpu.VMEM((1, rows), jnp.float32),
            pltpu.VMEM((calls, steps, lines, LANES), jnp.float32),
            pltpu.VMEM((calls, steps, lines, LANES), jnp.float32),
            pltpu.SemaphoreType.DMA((calls, steps)),
            pltpu.SemaphoreType.DMA((calls, steps)),
        ],
        compiler_params=pltpu.CompilerParams(
            collective_id=0, has_side_effects=True, vmem_limit_bytes=40 << 20
        ),
        name="fit_fixed",
    )(
        features,
        labels.reshape(1, rows),
        offsets.reshape(1, rows),
        feature_scale.reshape(lines, LANES),
        w_start.reshape(lines, LANES),
    )


def three_parts(value):
    first = value.astype(jnp.bfloat16)
    rest = value - first.astype(jnp.float32)
    second = rest.astype(jnp.bfloat16)
    third = (rest - second.astype(jnp.float32)).astype(jnp.bfloat16)
    return first, second, third


def invert_blocks(blocks):
    lane = lax.broadcasted_iota(jnp.int32, (BLOCK, LANES), 1)
    sub = lax.broadcasted_iota(jnp.int32, (BLOCK, LANES), 0)
    base = lane // BLOCK * BLOCK
    place = lane % BLOCK
    for k in range(BLOCK):
        here = place == k
        new = []
        for value in blocks:
            column = jnp.take_along_axis(value, base + k, axis=1)
            pivot = 1.0 / column[k : k + 1, :]
            row = jnp.where(here[k : k + 1, :], pivot, value[k : k + 1, :] * pivot)
            value = jnp.where(here, 0.0, value) - column * row
            new.append(jnp.where(sub == k, row, value))
        blocks = new
    return blocks


def member_kernel(z_ref, zt_ref, curv_ref, resid_ref, local_ref, coef_ref, score_ref, gram, upper, lower):
    width = z_ref.shape[1]
    slots = z_ref.shape[0]
    count = coef_ref.shape[0]
    per = LANES // BLOCK
    blocks = width // BLOCK
    local = local_ref[...]
    weighted = zt_ref[...].astype(jnp.float32) * curv_ref[...]
    first = weighted.astype(jnp.bfloat16)
    upper[...] = first
    lower[...] = (weighted - first.astype(jnp.float32)).astype(jnp.bfloat16)
    eye = (
        lax.broadcasted_iota(jnp.int32, (width, width), 0)
        == lax.broadcasted_iota(jnp.int32, (width, width), 1)
    ).astype(jnp.float32)

    @pl.loop(0, count)
    def _(m):
        mask = jnp.where(local == m.astype(jnp.float32), 1.0, 0.0).astype(jnp.bfloat16)
        total = lax.dot_general(
            upper[...] * mask, z_ref[...], NN, preferred_element_type=jnp.float32
        ) + lax.dot_general(
            lower[...] * mask, z_ref[...], NN, preferred_element_type=jnp.float32
        )
        gram[m] = total + ridge_member * eye

    member = lax.broadcasted_iota(jnp.int32, (count, slots), 0).astype(jnp.float32)
    own = member == local
    masked = jnp.where(own, resid_ref[...], 0.0)
    high = masked.astype(jnp.bfloat16)
    low = (masked - high.astype(jnp.float32)).astype(jnp.bfloat16)
    grad = lax.dot_general(
        high, z_ref[...], NN, preferred_element_type=jnp.float32
    ) + lax.dot_general(low, z_ref[...], NN, preferred_element_type=jnp.float32)
    rhs = [grad[m : m + 1, :] for m in range(count)]
    exact = dict(preferred_element_type=jnp.float32, precision=lax.Precision.HIGHEST)
    inverse_of = []
    heads = {}
    for b in range(blocks):
        lo, hi = b * BLOCK, (b + 1) * BLOCK
        squares = [gram[m, lo:hi, lo:hi] for m in range(count)]
        packed = [
            jnp.concatenate(squares[at : at + per], axis=1) for at in range(0, count, per)
        ]
        packed = invert_blocks(packed)
        inverses = [
            packed[m // per][:, m % per * BLOCK : (m % per + 1) * BLOCK] for m in range(count)
        ]
        panels = []
        if hi < width:
            for m in range(count):
                right = gram[m, lo:hi, hi:width]
                panel = lax.dot_general(inverses[m], right, NN, **exact)
                panels.append(panel)
                a1, a2, a3 = three_parts(right)
                b1, b2, b3 = three_parts(panel)
                left_cat = jnp.concatenate([a1, a1, a2, a2, a1, a3], axis=0)
                right_cat = jnp.concatenate([b1, b2, b1, b2, b3, b1], axis=0)
                gram[m, hi:width, hi:width] = gram[m, hi:width, hi:width] - lax.dot_general(
                    left_cat, right_cat, TN, preferred_element_type=jnp.float32
                )
                now = rhs[m]
                heads[(m, b)] = now[:, :BLOCK]
                rhs[m] = now[:, BLOCK:] - lax.dot_general(now[:, :BLOCK], panel, NN, **exact)
        else:
            for m in range(count):
                heads[(m, b)] = rhs[m]
        inverse_of.append((inverses, panels))
    solved = []
    for m in range(count):
        tail = None
        for b in reversed(range(blocks)):
            inverses, panels = inverse_of[b]
            part = lax.dot_general(heads[(m, b)], inverses[m], NN, **exact)
            if tail is not None:
                part = part - lax.dot_general(tail, panels[m], NT, **exact)
                tail = jnp.concatenate([part, tail], axis=1)
            else:
                tail = part
        solved.append(tail)
    coef = -jnp.concatenate(solved, axis=0)
    coef_ref[...] = coef
    high = coef.astype(jnp.bfloat16)
    low = (coef - high.astype(jnp.float32)).astype(jnp.bfloat16)
    scores = lax.dot_general(
        high, zt_ref[...], NN, preferred_element_type=jnp.float32
    ) + lax.dot_general(low, zt_ref[...], NN, preferred_element_type=jnp.float32)
    score_ref[...] = jnp.sum(jnp.where(own, scores, 0.0), axis=0, keepdims=True)


def fit_members(received, curv, resid, local):
    slots, width = received.shape
    whole = pl.BlockSpec(memory_space=pltpu.VMEM)
    return pl.pallas_call(
        member_kernel,
        out_shape=(
            jax.ShapeDtypeStruct((MEM_DEV, width), jnp.float32),
            jax.ShapeDtypeStruct((1, slots), jnp.float32),
        ),
        in_specs=[whole] * 5,
        out_specs=(whole,) * 2,
        scratch_shapes=[
            pltpu.VMEM((MEM_DEV, width, width), jnp.float32),
            pltpu.VMEM((width, slots), jnp.bfloat16),
            pltpu.VMEM((width, slots), jnp.bfloat16),
        ],
        compiler_params=pltpu.CompilerParams(vmem_limit_bytes=48 << 20),
        name="fit_members",
    )(received, received.T, curv, resid, local)


def on_device(n_grp, n_mem, features, re_features, member_id, slot, labels, offsets, feature_scale, w_start):
    row_count = features.shape[0]
    slots_all = 2 * row_count
    packed = jnp.zeros((slots_all, re_features.shape[1]), jnp.bfloat16).at[slot].set(re_features)
    received = lax.all_to_all(packed, "mem", split_axis=0, concat_axis=0, tiled=True)
    weights, curvature, resid_row = fit_fixed(
        features, labels, offsets, feature_scale, w_start, n_grp, n_mem
    )
    local_id = (member_id % MEM_DEV).astype(jnp.float32)
    row_weights = jnp.concatenate([curvature, resid_row, local_id[None, :]], axis=0)
    weight_slots = jnp.zeros((3, slots_all), jnp.float32).at[:, slot].set(row_weights)
    arrived = lax.all_to_all(weight_slots, "mem", split_axis=1, concat_axis=1, tiled=True)
    member_coef, slot_scores = fit_members(received, arrived[0:1], arrived[1:2], arrived[2:3])
    returned = lax.all_to_all(slot_scores[0], "mem", split_axis=0, concat_axis=0, tiled=True)
    row_offsets = returned[slot]
    return (weights.reshape(-1), member_coef, row_offsets)


def solution(mesh):
    placed = (
        P(("grp", "mem"), None),
        P(("grp", "mem"), None),
        P(("grp", "mem")),
        P(("grp", "mem")),
        P(("grp", "mem")),
        P(("grp", "mem")),
        P(),
        P(),
    )
    return jax.shard_map(
        functools.partial(on_device, mesh.shape["grp"], mesh.shape["mem"]),
        mesh=mesh,
        in_specs=placed,
        out_specs=(P(), P(("grp", "mem"), None), P(("grp", "mem"))),
        check_vma=False,
    )
```

time: 991 us -> 265 us (0.27)
  other arithmetic: 452 us -> 1.41 us
  blocking collectives: 333 us -> 0 us
  Pallas kernels: 0 us -> 187 us
  matrix products: 113 us -> 0 us
  between operations: 15.2 us -> 0.7 us
    another operation x16 -> x0, other arithmetic: 435 us -> none  [the longest x9 273 us: fit_members(): factor = jnp.linalg.cholesky(gram_all)]
    psum x8 -> x0, blocking collectives: 324 us -> none  [the longest x6 241 us: hessian_times(): summed = lax.psum(apply_columns(features, inner), ('grp', 'mem'))]
    pallas_call x0 -> x2, Pallas kernels: none -> 187 us  [the longest x1 134 us: fit_fixed(): pl.pallas_call(functools.partial(fit_kernel, n_grp, n_mem), out_shape=(li...]
    dot_general x37 -> x0, matrix products: 100 us -> none  [the longest x9 51.3 us: apply_rows(): jnp.dot(features, split_two(vector), preferred_element_type=jnp.float32)]
    another operation x8 -> x0, matrix products: 12.6 us -> none  [the longest x6 7.68 us: fit_members(): jax.scipy.linalg.cho_solve((factor, True), member_grad[:, :, None])[:, :, 0]]
  transfers between devices with their start and end apart: 2 -> 3, of which waited for: 2 -> 2; matrix products, arithmetic and copies ran while one was open for 1% -> 3% of each run, Pallas kernels for 0% -> 0%
where the time goes in v1:
time: 265 us; the launch traced here: 264 us
  Pallas kernels  187 us (71%)
  waiting for transfers between devices  31.6 us (12%)
  local copies, waits for them, and re-layouts  29.4 us (11%)
  starting transfers between devices  14.3 us (5%)
    pallas_call x1, Pallas kernels, fit_fixed(): pl.pallas_call(functools.partial(fit_kernel, n_grp, n_mem), out_shape=(li...  134 us
    pallas_call x1, Pallas kernels, fit_members(): pl.pallas_call(member_kernel, out_shape=(jax.ShapeDtypeStruct((MEM_DEV, w...  53 us
    all_to_all x1, waiting for transfers between devices, on_device(): lax.all_to_all(packed, 'mem', split_axis=0, concat_axis=0, tiled=True)  25 us
    gather x1, local copies, waits for them, and re-layouts, on_device(): row_offsets = returned[slot]  10.5 us
    unnamed x11, local copies, waits for them, and re-layouts  6.79 us
    all_to_all x1, waiting for transfers between devices, on_device(): lax.all_to_all(slot_scores[0], 'mem', split_axis=0, concat_axis=0, tiled=...  6.52 us
    all_to_all x1, starting transfers between devices, on_device(): lax.all_to_all(packed, 'mem', split_axis=0, concat_axis=0, tiled=True)  6 us
    scatter x1, local copies, waits for them, and re-layouts, on_device(): jnp.zeros((slots_all, re_features.shape[1]), jnp.bfloat16).at[slot]  5.67 us
  transfers between devices with their start and end apart: 3, of which 2 were waited for; matrix products, arithmetic and copies ran while one was open for 3% of the time, Pallas kernels for 0%

profile of v1, /device:TPU:0, one launch (start us, length us, event | category | flops | bytes accessed | tf_op | source)
XLA Modules:
  0.0 264.1 jit_solution(214039533699273822)
XLA Ops:
  0.6 0.7 fusion.5
  1.3 0.7 broadcast_clamp_fusion
  2.0 3.4 %copy-done = bf16[1024,4096]{1,0:T(8,128)(2,1)S(1)} copy-done((bf16[1024,4096]{1,0:T(8,128)(2,1)S(1)}, bf16[1024,4096]{1,0:T(8,128)(2,1)}, u32[]{:S(2)}) %copy-start) | copy-done | bytes 8388632
  5.4 0.7 copy-done.1
  6.1 0.7 copy-done.2
  6.8 0.7 copy-done.3
  7.5 0.7 copy-done.4
  8.2 133.7 %fit_fixed.1 = (f32[32,128]{1,0:T(8,128)S(1)}, f32[1,1024]{1,0:T(1,128)S(1)}, f32[1,1024]{1,0:T(1,128)S(1)}) custom-call(bf16[1024,4096]{1,0:T(8,128)(2,1)S(1)} %copy-done, s32[1,1024]{1,0:T(1,128)S(1)} %bitcast.29, f32[1,1024]{1,0:T(1,128)S(1)} %bitcast.30, f32[32,128]{1,0:T(8,128)S(1)} %bitcast.26, f32[32,128]{1,0:T(8,128)S(1)} %bitcast.27), custom_call_target="tpu_custom_call" | custom-call | tf_op jit(solution)/shard_map/fit_fixed/pallas_call | solution.py:149
  141.9 0.2 copy.20
  142.2 3.3 %scatter_custom_fusion.1 = f32[3,2048]{0,1:T(8,128)S(1)} fusion(s32[1024]{0:T(1024)S(1)} %get-tuple-element.17, f32[1024,3]{1,0:T(8,128)S(1)} %copy.20, f32[]{:T(128)} %constant.19.clone.1), kind=kCustom, calls=%fused_computation.3 | custom fusion | bytes 24580 | tf_op jit(solution)/shard_map/scatter | solution.py:322
  145.5 0.9 copy.21
  146.4 4.9 %all-to-all-start.1 = ((f32[3,8,256]{2,0,1:T(4,128)}), f32[3,8,256]{2,0,1:T(4,128)S(1)}, u32[]{:S(2)}, u32[]{:S(2)}) async-start(f32[3,8,256]{2,0,1:T(4,128)} %copy.21), calls=%async_computation.1 | async-start | bytes 65536 | tf_op jit(solution)/shard_map/all_to_all | solution.py:323
  151.3 5.7 %scatter_custom_fusion = bf16[2048,256]{1,0:T(8,128)(2,1)S(1)} fusion(s32[1024]{0:T(1024)S(1)} %get-tuple-element.17, bf16[1024,256]{1,0:T(8,128)(2,1)} %param.9, bf16[]{:T(256)} %constant.16.clone.1), kind=kCustom, calls=%fused_computation.5 | custom fusion | bytes 1049088 | tf_op jit(solution)/shard_map/scatter | solution.py:315
  157.0 1.3 copy.18
  158.3 0.0 all-to-all-done.1
  158.3 6.0 %all-to-all-start = ((bf16[8,256,256]{1,2,0:T(8,128)(2,1)}), bf16[8,256,256]{1,2,0:T(8,128)(2,1)S(1)}, u32[]{:S(2)}, u32[]{:S(2)}) async-start(bf16[8,256,256]{1,2,0:T(8,128)(2,1)} %copy.18), calls=%async_computation | async-start | bytes 2097152 | tf_op jit(solution)/shard_map/all_to_all | solution.py:316
  164.3 25.0 %all-to-all-done = bf16[8,256,256]{1,2,0:T(8,128)(2,1)S(1)} async-done(((bf16[8,256,256]{1,2,0:T(8,128)(2,1)}), bf16[8,256,256]{1,2,0:T(8,128)(2,1)S(1)}, u32[]{:S(2)}, u32[]{:S(2)}) %all-to-all-start) | async-done | bytes 1048608 | tf_op jit(solution)/shard_map/all_to_all | solution.py:316
  189.4 0.1 copy.24
  189.5 0.5 copy.22.z_ref
  190.0 53.0 %fit_members.1 = (f32[8,256]{1,0:T(8,128)}, f32[1,2048]{1,0:T(1,128)}) custom-call(bf16[2048,256]{1,0:T(8,128)(2,1)S(1)} %copy.22.z_ref, bf16[256,2048]{1,0:T(8,128)(2,1)S(1)} %bitcast.22, f32[1,2048]{1,0:T(1,128)S(1)} %bitcast.25, f32[1,2048]{1,0:T(1,128)S(1)} %bitcast.24, f32[1,2048]{1,0:T(1,128)S(1)} %bitcast.23), custom_call_target="tpu_custom_call" | custom-call | tf_op jit(solution)/shard_map/fit_members/pallas_call | solution.py:294
  243.1 3.4 %all-to-all-start.2 = ((f32[8,256,1]{1,2,0:T(1,128)}), f32[8,256,1]{1,2,0:T(1,128)S(1)}, u32[]{:S(2)}, u32[]{:S(2)}) async-start(f32[8,256,1]{1,2,0:T(1,128)} %bitcast.13), calls=%async_computation.2 | async-start | bytes 16384 | tf_op jit(solution)/shard_map/all_to_all | solution.py:325
  246.4 6.5 %all-to-all-done.2 = f32[8,256,1]{1,2,0:T(1,128)S(1)} async-done(((f32[8,256,1]{1,2,0:T(1,128)}), f32[8,256,1]{1,2,0:T(1,128)S(1)}, u32[]{:S(2)}, u32[]{:S(2)}) %all-to-all-start.2) | async-done | bytes 8224 | tf_op jit(solution)/shard_map/all_to_all | solution.py:325
  253.0 10.5 %gather_fusion = f32[1024]{0:T(1024)} fusion(f32[2048]{0:T(1024)S(1)} %bitcast.31, s32[1024]{0:T(1024)S(1)} %get-tuple-element.16), kind=kCustom, calls=%fused_computation | custom fusion | bytes 12288 | tf_op jit(solution)/shard_map/gather | solution.py:326
  263.5 0.6 copy.26
  (7 shorter events, 0.0 us)
Async XLA Ops:
  2.0 3.4 %copy-start = (bf16[1024,4096]{1,0:T(8,128)(2,1)S(1)}, bf16[1024,4096]{1,0:T(8,128)(2,1)}, u32[]{:S(2)}) copy-start(bf16[1024,4096]{1,0:T(8,128)(2,1)} %feat.1) | copy-start | bytes 25165828
  5.4 0.7 copy-start.1
  6.1 0.7 copy-start.2
  6.8 0.7 copy-start.3
  7.5 0.7 copy-start.4
  146.4 11.9 %all-to-all-start.1 = ((f32[3,8,256]{2,0,1:T(4,128)}), f32[3,8,256]{2,0,1:T(4,128)S(1)}, u32[]{:S(2)}, u32[]{:S(2)}) async-start(f32[3,8,256]{2,0,1:T(4,128)} %copy.21), calls=%async_computation.1 | async-start | bytes 65536 | tf_op jit(solution)/shard_map/all_to_all | solution.py:323
  158.3 31.1 %all-to-all-start = ((bf16[8,256,256]{1,2,0:T(8,128)(2,1)}), bf16[8,256,256]{1,2,0:T(8,128)(2,1)S(1)}, u32[]{:S(2)}, u32[]{:S(2)}) async-start(bf16[8,256,256]{1,2,0:T(8,128)(2,1)} %copy.18), calls=%async_computation | async-start | bytes 2097152 | tf_op jit(solution)/shard_map/all_to_all | solution.py:316
  243.1 9.9 %all-to-all-start.2 = ((f32[8,256,1]{1,2,0:T(1,128)}), f32[8,256,1]{1,2,0:T(1,128)S(1)}, u32[]{:S(2)}, u32[]{:S(2)}) async-start(f32[8,256,1]{1,2,0:T(1,128)} %bitcast.13), calls=%async_computation.2 | async-start | bytes 16384 | tf_op jit(solution)/shard_map/all_to_all | solution.py:325

commit v2 on v1

v2 whole, which is shorter than its diff:
```python
import functools

import jax
import jax.numpy as jnp
from jax import lax
from jax.experimental import pallas as pl
from jax.experimental.pallas import tpu as pltpu
from jax.sharding import PartitionSpec as P

MEM_DEV = 8
NEWTON = 2
CG_ITERS = 3
LANES = 128
BLOCK = 32

ridge_fixed = 1.0
ridge_member = 1.0
MESH_ID = pl.DeviceIdType.MESH
NT = (((1,), (1,)), ((), ()))
NN = (((1,), (0,)), ((), ()))
TN = (((0,), (0,)), ((), ()))


def pair_rows(row):
    upper = row.astype(jnp.bfloat16).astype(jnp.float32)
    lower = (row - upper).astype(jnp.bfloat16).astype(jnp.float32)
    at = lax.broadcasted_iota(jnp.int32, (16, row.shape[1]), 0)
    both = jnp.where(at == 0, upper, jnp.where(at == 1, lower, 0.0))
    return both.astype(jnp.bfloat16)


def three_parts(value):
    first = value.astype(jnp.bfloat16)
    rest = value - first.astype(jnp.float32)
    second = rest.astype(jnp.bfloat16)
    third = (rest - second.astype(jnp.float32)).astype(jnp.bfloat16)
    return first, second, third


def invert_blocks(blocks):
    lane = lax.broadcasted_iota(jnp.int32, (BLOCK, LANES), 1)
    sub = lax.broadcasted_iota(jnp.int32, (BLOCK, LANES), 0)
    base = lane // BLOCK * BLOCK
    place = lane % BLOCK
    for k in range(BLOCK):
        here = place == k
        new = []
        for value in blocks:
            column = jnp.take_along_axis(value, base + k, axis=1)
            pivot = 1.0 / column[k : k + 1, :]
            row = jnp.where(here[k : k + 1, :], pivot, value[k : k + 1, :] * pivot)
            value = jnp.where(here, 0.0, value) - column * row
            new.append(jnp.where(sub == k, row, value))
        blocks = new
    return blocks


def fit_members(z_ref, zt_ref, curv_row, resid_row, local, coef_ref, gram, upper, lower):
    width = z_ref.shape[1]
    slots = z_ref.shape[0]
    count = coef_ref.shape[0]
    per = LANES // BLOCK
    blocks = width // BLOCK
    weighted = zt_ref[...].astype(jnp.float32) * curv_row
    first = weighted.astype(jnp.bfloat16)
    upper[...] = first
    lower[...] = (weighted - first.astype(jnp.float32)).astype(jnp.bfloat16)
    eye = (
        lax.broadcasted_iota(jnp.int32, (width, width), 0)
        == lax.broadcasted_iota(jnp.int32, (width, width), 1)
    ).astype(jnp.float32)

    @pl.loop(0, count)
    def _(m):
        mask = jnp.where(local == m.astype(jnp.float32), 1.0, 0.0).astype(jnp.bfloat16)
        total = lax.dot_general(
            upper[...] * mask, z_ref[...], NN, preferred_element_type=jnp.float32
        ) + lax.dot_general(
            lower[...] * mask, z_ref[...], NN, preferred_element_type=jnp.float32
        )
        gram[m] = total + ridge_member * eye

    member = lax.broadcasted_iota(jnp.int32, (count, slots), 0).astype(jnp.float32)
    own = member == local
    masked = jnp.where(own, resid_row, 0.0)
    high = masked.astype(jnp.bfloat16)
    low = (masked - high.astype(jnp.float32)).astype(jnp.bfloat16)
    grad = lax.dot_general(
        high, z_ref[...], NN, preferred_element_type=jnp.float32
    ) + lax.dot_general(low, z_ref[...], NN, preferred_element_type=jnp.float32)
    rhs = [grad[m : m + 1, :] for m in range(count)]
    exact = dict(preferred_element_type=jnp.float32, precision=lax.Precision.HIGHEST)
    inverse_of = []
    heads = {}
    for b in range(blocks):
        lo, hi = b * BLOCK, (b + 1) * BLOCK
        squares = [gram[m, lo:hi, lo:hi] for m in range(count)]
        packed = [
            jnp.concatenate(squares[at : at + per], axis=1) for at in range(0, count, per)
        ]
        packed = invert_blocks(packed)
        inverses = [
            packed[m // per][:, m % per * BLOCK : (m % per + 1) * BLOCK] for m in range(count)
        ]
        panels = []
        if hi < width:
            for m in range(count):
                right = gram[m, lo:hi, hi:width]
                panel = lax.dot_general(inverses[m], right, NN, **exact)
                panels.append(panel)
                a1, a2, a3 = three_parts(right)
                b1, b2, b3 = three_parts(panel)
                left_cat = jnp.concatenate([a1, a1, a2, a2, a1, a3], axis=0)
                right_cat = jnp.concatenate([b1, b2, b1, b2, b3, b1], axis=0)
                gram[m, hi:width, hi:width] = gram[m, hi:width, hi:width] - lax.dot_general(
                    left_cat, right_cat, TN, preferred_element_type=jnp.float32
                )
                now = rhs[m]
                heads[(m, b)] = now[:, :BLOCK]
                rhs[m] = now[:, BLOCK:] - lax.dot_general(now[:, :BLOCK], panel, NN, **exact)
        else:
            for m in range(count):
                heads[(m, b)] = rhs[m]
        inverse_of.append((inverses, panels))
    solved = []
    for m in range(count):
        tail = None
        for b in reversed(range(blocks)):
            inverses, panels = inverse_of[b]
            part = lax.dot_general(heads[(m, b)], inverses[m], NN, **exact)
            if tail is not None:
                part = part - lax.dot_general(tail, panels[m], NT, **exact)
                tail = jnp.concatenate([part, tail], axis=1)
            else:
                tail = part
        solved.append(tail)
    coef = -jnp.concatenate(solved, axis=0)
    coef_ref[...] = coef
    high = coef.astype(jnp.bfloat16)
    low = (coef - high.astype(jnp.float32)).astype(jnp.bfloat16)
    scores = lax.dot_general(
        high, zt_ref[...], NN, preferred_element_type=jnp.float32
    ) + lax.dot_general(low, zt_ref[...], NN, preferred_element_type=jnp.float32)
    return jnp.sum(jnp.where(own, scores, 0.0), axis=0, keepdims=True)


def window_kernel(
    n_grp, n_mem,
    feat_hbm, re_hbm, member_hbm, slot_hbm, label_hbm, offset_hbm, scale_hbm, start_hbm,
    weight_ref, coef_ref, offsets_ref,
    feat, re_ref, member_ref, slot_ref, label_ref, offset_ref, scale_ref, vec_w,
    vec_u, vec_r, vec_p, curv, send, recv,
    pick, z_send, z_ref, zs_ref, zt_ref, w_send, w_recv, s_send, s_recv, gram, upper, lower, row_vals,
    load_sem, feat_sem, send_sem, recv_sem, zs_sem, zr_sem, ws_sem, wr_sem, ss_sem, sr_sem,
):
    rows, width = feat.shape
    lines = width // LANES
    slots = z_ref.shape[0]
    cap = slots // n_mem
    calls = NEWTON * (CG_ITERS + 1)
    each = n_mem // calls
    me_grp = lax.axis_index("grp")
    me_mem = lax.axis_index("mem")

    loads = [
        pltpu.make_async_copy(source, target, load_sem.at[i])
        for i, (source, target) in enumerate(
            (
                (scale_hbm, scale_ref), (start_hbm, vec_w), (offset_hbm, offset_ref),
                (label_hbm, label_ref), (slot_hbm, slot_ref), (member_hbm, member_ref),
                (re_hbm, re_ref),
            )
        )
    ]
    feat_loads = [
        pltpu.make_async_copy(
            feat_hbm.at[pl.ds(first, 256)], feat.at[pl.ds(first, 256)], feat_sem.at[first // 256]
        )
        for first in range(0, rows, 256)
    ]
    for load in loads[:4] + feat_loads + loads[4:]:
        load.start()

    partners = []
    for name, me, size in (("mem", me_mem, n_mem), ("grp", me_grp, n_grp)):
        bit = 1
        while bit < size:
            other = me + bit * (1 - 2 * ((me // bit) % 2))
            partners.append((me_grp, other) if name == "mem" else (other, me_mem))
            bit *= 2

    barrier = pltpu.get_barrier_semaphore()
    for turn in range(1, n_mem):
        pl.semaphore_signal(
            barrier, inc=1, device_id=(me_grp, lax.rem(me_mem + turn, n_mem)), device_id_type=MESH_ID
        )
    for partner in partners[n_mem.bit_length() - 1 :]:
        pl.semaphore_signal(barrier, inc=1, device_id=partner, device_id_type=MESH_ID)
    pl.semaphore_wait(barrier, n_mem - 1 + n_grp.bit_length() - 1)
    for load in loads[:4]:
        load.wait()

    def peer(turn):
        return (me_grp, lax.rem(me_mem + turn, n_mem))

    def z_copy(turn):
        return pltpu.make_async_remote_copy(
            src_ref=z_send.at[turn - 1],
            dst_ref=z_ref.at[pl.ds(pl.multiple_of(me_mem * cap, cap), cap)],
            send_sem=zs_sem.at[turn - 1],
            recv_sem=zr_sem.at[turn - 1],
            device_id=peer(turn),
            device_id_type=MESH_ID,
        )

    def build(turn):
        first = pl.multiple_of(lax.rem(me_mem + turn, n_mem) * cap, cap)
        at = lax.broadcasted_iota(jnp.int32, (cap, rows), 0) + first
        chosen = jnp.where(at == slot_ref[...], 1.0, 0.0).astype(jnp.bfloat16)
        pick[pl.ds(first, cap), :] = chosen
        block = lax.dot_general(chosen, re_ref[...], NN, preferred_element_type=jnp.float32)
        block = block.astype(jnp.bfloat16)

        @pl.when(turn < n_mem)
        def _():
            z_send[turn - 1] = block

        @pl.when(turn == n_mem)
        def _():
            z_ref[pl.ds(pl.multiple_of(me_mem * cap, cap), cap), :] = block

    def all_sum(value, call):
        for step, partner in enumerate(partners):
            send[call, step] = value
            copy = pltpu.make_async_remote_copy(
                src_ref=send.at[call, step],
                dst_ref=recv.at[call, step],
                send_sem=send_sem.at[call, step],
                recv_sem=recv_sem.at[call, step],
                device_id=partner,
                device_id_type=MESH_ID,
            )
            copy.start()
            if step == 0:
                for q in range(each):
                    build(1 + call * each + q)
            copy.wait()
            value = value + recv[call, step]
        for q in range(each):
            turn = 1 + call * each + q

            @pl.when(turn < n_mem)
            def _():
                z_copy(turn).start()

        return value

    def times_rows(vector, loading=None):
        row = jnp.concatenate([vector[i : i + 1, :] for i in range(lines)], axis=1)
        pair = pair_rows(row)
        parts = []
        for first in range(0, rows, 256):
            if loading is not None:
                @pl.when(loading == 0)
                def _():
                    feat_loads[first // 256].wait()
            got = lax.dot_general(
                pair, feat[first : first + 256, :], NT, preferred_element_type=jnp.float32
            )
            parts.append(got[0:1] + got[1:2])
        return jnp.concatenate(parts, axis=1)

    def times_columns(row):
        pair = pair_rows(row)
        parts = []
        for first in range(0, width, 256):
            got = lax.dot_general(
                pair, feat[:, first : first + 256], NN, preferred_element_type=jnp.float32
            )
            got = got[0:1] + got[1:2]
            parts += [got[:, at : at + LANES] for at in range(0, 256, LANES)]
        return jnp.concatenate(parts, axis=0)

    def total(value):
        return jnp.sum(jnp.sum(value, axis=1, keepdims=True), axis=0, keepdims=True)

    scale = scale_ref[...]
    target = label_ref[...].astype(jnp.float32)

    def newton(step, carry):
        base = step * (CG_ITERS + 1)
        weights = vec_w[...]
        margin = times_rows(scale * weights, step) + offset_ref[...]
        prob = 1.0 / (1.0 + jnp.exp(-margin))
        curv[...] = prob * (1.0 - prob)
        grad = times_columns(prob - target)

        @pl.when(step == 0)
        def _():
            for load in loads[4:]:
                load.wait()

        summed = all_sum(grad, base)
        resid = -(scale * summed + ridge_fixed * weights)
        vec_r[...] = resid
        vec_p[...] = resid
        vec_u[...] = jnp.zeros_like(resid)

        def cg(k, norm):
            direction = vec_p[...]
            inner = curv[...] * times_rows(scale * direction)
            image = scale * all_sum(times_columns(inner), base + 1 + k) + ridge_fixed * direction
            size = norm / total(direction * image)
            vec_u[...] = vec_u[...] + size * direction
            left = vec_r[...] - size * image
            vec_r[...] = left
            new_norm = total(left * left)
            vec_p[...] = left + new_norm / norm * direction
            return new_norm

        lax.fori_loop(0, CG_ITERS, cg, total(resid * resid))
        vec_w[...] = weights + vec_u[...]
        return carry

    lax.fori_loop(0, NEWTON, newton, 0)
    weights = vec_w[...]
    weight_ref[...] = weights
    score = times_rows(scale * weights)
    prob = 1.0 / (1.0 + jnp.exp(-score))
    local_id = lax.rem(member_ref[...], MEM_DEV).astype(jnp.float32)
    row_vals[...] = jnp.zeros_like(row_vals)
    row_vals[0:1, :] = prob * (1.0 - prob)
    row_vals[1:2, :] = prob - target
    row_vals[2:3, :] = local_id
    parts = jnp.concatenate([p.astype(jnp.float32) for p in three_parts(row_vals[...])], axis=0)
    parts = jnp.concatenate([parts, jnp.zeros_like(parts[0:8])], axis=0).astype(jnp.bfloat16)

    def small_copy(source, target, turn, sends, recvs):
        return pltpu.make_async_remote_copy(
            src_ref=source.at[turn - 1],
            dst_ref=target.at[turn - 1],
            send_sem=sends.at[turn - 1],
            recv_sem=recvs.at[turn - 1],
            device_id=peer(turn),
            device_id_type=MESH_ID,
        )

    for turn in range(1, n_mem + 1):
        first = pl.multiple_of(lax.rem(me_mem + turn, n_mem) * cap, cap)
        got = lax.dot_general(
            parts, pick[pl.ds(first, cap), :], NT, preferred_element_type=jnp.float32
        )
        got = got[0:8] + got[8:16] + got[16:24]
        if turn < n_mem:
            w_send[turn - 1] = got
            small_copy(w_send, w_recv, turn, ws_sem, wr_sem).start()
        else:
            w_recv[n_mem - 1] = got
    for turn in range(1, n_mem):
        z_copy(turn).wait()
    for turn in range(1, n_mem + 1):
        source = lax.rem(me_mem + n_mem - turn, n_mem)
        block = z_ref[pl.ds(pl.multiple_of(source * cap, cap), cap), :]
        zt_ref[:, (turn - 1) * cap : turn * cap] = block.T
        zs_ref[(turn - 1) * cap : turn * cap, :] = block
    for turn in range(1, n_mem):
        small_copy(w_send, w_recv, turn, ws_sem, wr_sem).wait()
    arrived = jnp.concatenate([w_recv[t] for t in range(n_mem)], axis=1)
    scores = fit_members(
        zs_ref, zt_ref, arrived[0:1], arrived[1:2], arrived[2:3], coef_ref, gram, upper, lower
    )
    for turn in range(1, n_mem + 1):
        back = jnp.broadcast_to(scores[:, (turn - 1) * cap : turn * cap], (8, cap))
        if turn < n_mem:
            s_send[n_mem - turn - 1] = back
        else:
            s_recv[n_mem - 1] = back
    for turn in range(1, n_mem):
        small_copy(s_send, s_recv, turn, ss_sem, sr_sem).start()
    for turn in range(1, n_mem):
        small_copy(s_send, s_recv, turn, ss_sem, sr_sem).wait()
    result = jnp.zeros((1, rows), jnp.float32)
    for turn in range(1, n_mem + 1):
        owner = lax.rem(me_mem + n_mem - turn, n_mem)
        value = s_recv[turn - 1][0:1]
        p1, p2, p3 = (p.astype(jnp.float32) for p in three_parts(value))
        at = lax.broadcasted_iota(jnp.int32, (16, cap), 0)
        stack = jnp.where(at == 0, p1, jnp.where(at == 1, p2, jnp.where(at == 2, p3, 0.0)))
        got = lax.dot_general(
            stack.astype(jnp.bfloat16),
            pick[pl.ds(pl.multiple_of(owner * cap, cap), cap), :],
            NN,
            preferred_element_type=jnp.float32,
        )
        result = result + (got[0:1] + got[1:2] + got[2:3])
    offsets_ref[...] = result


def on_device(n_grp, n_mem, features, re_features, member_id, slot, labels, offsets, feature_scale, w_start):
    rows, width = features.shape
    inner = re_features.shape[1]
    lines = width // LANES
    slots = 2 * rows
    cap = slots // n_mem
    steps = (n_grp.bit_length() - 1) + (n_mem.bit_length() - 1)
    calls = NEWTON * (CG_ITERS + 1)
    f32, bf16, i32 = jnp.float32, jnp.bfloat16, jnp.int32
    held = pltpu.VMEM((lines, LANES), f32)
    dma = pltpu.SemaphoreType.DMA
    whole = pl.BlockSpec(memory_space=pltpu.VMEM)
    weights, member_coef, row_offsets = pl.pallas_call(
        functools.partial(window_kernel, n_grp, n_mem),
        out_shape=(
            jax.ShapeDtypeStruct((lines, LANES), f32),
            jax.ShapeDtypeStruct((MEM_DEV, inner), f32),
            jax.ShapeDtypeStruct((1, rows), f32),
        ),
        in_specs=[pl.BlockSpec(memory_space=pl.ANY)] * 8,
        out_specs=(whole,) * 3,
        scratch_shapes=[
            pltpu.VMEM((rows, width), bf16),
            pltpu.VMEM((rows, inner), bf16),
            pltpu.VMEM((1, rows), i32),
            pltpu.VMEM((1, rows), i32),
            pltpu.VMEM((1, rows), i32),
            pltpu.VMEM((1, rows), f32),
            held, held, held, held, held,
            pltpu.VMEM((1, rows), f32),
            pltpu.VMEM((calls, steps, lines, LANES), f32),
            pltpu.VMEM((calls, steps, lines, LANES), f32),
            pltpu.VMEM((slots, rows), bf16),
            pltpu.VMEM((n_mem - 1, cap, inner), bf16),
            pltpu.VMEM((slots, inner), bf16),
            pltpu.VMEM((slots, inner), bf16),
            pltpu.VMEM((inner, slots), bf16),
            pltpu.VMEM((n_mem - 1, 8, cap), f32),
            pltpu.VMEM((n_mem, 8, cap), f32),
            pltpu.VMEM((n_mem - 1, 8, cap), f32),
            pltpu.VMEM((n_mem, 8, cap), f32),
            pltpu.VMEM((MEM_DEV, inner, inner), f32),
            pltpu.VMEM((inner, slots), bf16),
            pltpu.VMEM((inner, slots), bf16),
            pltpu.VMEM((8, rows), f32),
            dma((7,)),
            dma((rows // 256,)),
            dma((calls, steps)),
            dma((calls, steps)),
            dma((n_mem - 1,)),
            dma((n_mem - 1,)),
            dma((n_mem - 1,)),
            dma((n_mem - 1,)),
            dma((n_mem - 1,)),
            dma((n_mem - 1,)),
        ],
        compiler_params=pltpu.CompilerParams(
            collective_id=0, has_side_effects=True, vmem_limit_bytes=60 << 20
        ),
        name="window",
    )(
        features,
        re_features,
        member_id.reshape(1, rows),
        slot.reshape(1, rows),
        labels.reshape(1, rows),
        offsets.reshape(1, rows),
        feature_scale.reshape(lines, LANES),
        w_start.reshape(lines, LANES),
    )
    return (weights.reshape(-1), member_coef, row_offsets.reshape(-1))


def solution(mesh):
    placed = (
        P(("grp", "mem"), None),
        P(("grp", "mem"), None),
        P(("grp", "mem")),
        P(("grp", "mem")),
        P(("grp", "mem")),
        P(("grp", "mem")),
        P(),
        P(),
    )
    return jax.shard_map(
        functools.partial(on_device, mesh.shape["grp"], mesh.shape["mem"]),
        mesh=mesh,
        in_specs=placed,
        out_specs=(P(), P(("grp", "mem"), None), P(("grp", "mem"))),
        check_vma=False,
    )
```

time: 265 us -> 212 us (0.80)
  waiting for transfers between devices: 31.6 us -> 0 us
  local copies, waits for them, and re-layouts: 29.4 us -> 3.89 us
  Pallas kernels: 187 us -> 207 us
  starting transfers between devices: 14.3 us -> 0 us
    all_to_all x3 -> x0, waiting for transfers between devices: 31.6 us -> none  [the longest x1 25 us: on_device(): lax.all_to_all(packed, 'mem', split_axis=0, concat_axis=0, tiled=True)]
    pallas_call x2 -> x1, Pallas kernels: 187 us -> 207 us  [on_device(): pl.pallas_call(functools.partial(window_kernel, n_grp, n_mem), out_shape=...]
    all_to_all x3 -> x0, starting transfers between devices: 14.3 us -> none  [the longest x1 6 us: on_device(): lax.all_to_all(packed, 'mem', split_axis=0, concat_axis=0, tiled=True)]
    gather x1 -> x0, local copies, waits for them, and re-layouts: 10.5 us -> none  [on_device(): row_offsets = returned[slot]]
    scatter x2 -> x0, local copies, waits for them, and re-layouts: 9.01 us -> none  [the longest x1 5.67 us: on_device(): jnp.zeros((slots_all, re_features.shape[1]), jnp.bfloat16).at[slot]]
    unnamed x11 -> x3, local copies, waits for them, and re-layouts: 6.79 us -> 3.89 us
    all_to_all x4 -> x0, local copies, waits for them, and re-layouts: 2.87 us -> none  [the longest x3 1.94 us: on_device(): lax.all_to_all(packed, 'mem', split_axis=0, concat_axis=0, tiled=True)]
  transfers between devices with their start and end apart: 3 -> 0, of which waited for: 2 -> 0; matrix products, arithmetic and copies ran while one was open for 3% -> 0% of each run, Pallas kernels for 0% -> 0%
where the time goes in v2:
time: 212 us
  Pallas kernels  207 us (98%)
  local copies, waits for them, and re-layouts  3.89 us (2%)
    pallas_call x1, Pallas kernels, on_device(): pl.pallas_call(functools.partial(window_kernel, n_grp, n_mem), out_shape=...  207 us

profile of v2, /device:TPU:0, one launch (start us, length us, event | category | flops | bytes accessed | tf_op | source)
XLA Modules:
  0.0 211.7 jit_solution(2991953859082475935)
XLA Ops:
  0.6 207.1 %window.1 = (f32[32,128]{1,0:T(8,128)}, f32[8,256]{1,0:T(8,128)}, f32[1,1024]{1,0:T(1,128)}) custom-call(bf16[1024,4096]{1,0:T(8,128)(2,1)} %feat_hbm.1, bf16[1024,256]{1,0:T(8,128)(2,1)} %re_hbm.1, s32[1,1024]{1,0:T(1,128)} %bitcast.11, s32[1,1024]{1,0:T(1,128)} %bitcast.12, s32[1,1024]{1,0:T(1,128)} %bitcast.13, f32[1,1024]{1,0:T(1,128)} %bitcast.14, ...), custom_call_target="tpu_custom_call" | custom-call | tf_op jit(solution)/shard_map/window/pallas_call | solution.py:411
  207.8 1.3 copy.14
  209.1 1.3 copy.15
  210.4 1.3 copy.16

commit v3 on v2

--- a/solution.py
+++ b/solution.py
@@ -42,15 +42,23 @@
     sub = lax.broadcasted_iota(jnp.int32, (BLOCK, LANES), 0)
     base = lane // BLOCK * BLOCK
     place = lane % BLOCK
-    for k in range(BLOCK):
-        here = place == k
+    for k in range(0, BLOCK, 2):
+        one, two = place == k, place == k + 1
         new = []
         for value in blocks:
-            column = jnp.take_along_axis(value, base + k, axis=1)
-            pivot = 1.0 / column[k : k + 1, :]
-            row = jnp.where(here[k : k + 1, :], pivot, value[k : k + 1, :] * pivot)
-            value = jnp.where(here, 0.0, value) - column * row
-            new.append(jnp.where(sub == k, row, value))
+            left = jnp.take_along_axis(value, base + k, axis=1)
+            right = jnp.take_along_axis(value, base + k + 1, axis=1)
+            a, b = left[k : k + 1, :], right[k : k + 1, :]
+            c, d = left[k + 1 : k + 2, :], right[k + 1 : k + 2, :]
+            inverse = 1.0 / (a * d - b * c)
+            a, b, c, d = d * inverse, -b * inverse, -c * inverse, a * inverse
+            top, low = value[k : k + 1, :], value[k + 1 : k + 2, :]
+            at_one, at_two = one[0:1, :], two[0:1, :]
+            first = jnp.where(at_one, a, jnp.where(at_two, b, a * top + b * low))
+            second = jnp.where(at_one, c, jnp.where(at_two, d, c * top + d * low))
+            value = jnp.where(one | two, 0.0, value) - left * first - right * second
+            value = jnp.where(sub == k, first, jnp.where(sub == k + 1, second, value))
+            new.append(value)
         blocks = new
     return blocks
 
@@ -149,9 +157,9 @@
     feat_hbm, re_hbm, member_hbm, slot_hbm, label_hbm, offset_hbm, scale_hbm, start_hbm,
     weight_ref, coef_ref, offsets_ref,
     feat, re_ref, member_ref, slot_ref, label_ref, offset_ref, scale_ref, vec_w,
-    vec_u, vec_r, vec_p, curv, send, recv,
+    vec_u, vec_r, vec_p, curv, near_send, near_recv, far_send, far_recv,
     pick, z_send, z_ref, zs_ref, zt_ref, w_send, w_recv, s_send, s_recv, gram, upper, lower, row_vals,
-    load_sem, feat_sem, send_sem, recv_sem, zs_sem, zr_sem, ws_sem, wr_sem, ss_sem, sr_sem,
+    load_sem, feat_sem, ns_sem, nr_sem, fs_sem, fr_sem, zs_sem, zr_sem, ws_sem, wr_sem, ss_sem, sr_sem,
 ):
     rows, width = feat.shape
     lines = width // LANES
@@ -181,22 +189,28 @@
     for load in loads[:4] + feat_loads + loads[4:]:
         load.start()
 
-    partners = []
-    for name, me, size in (("mem", me_mem, n_mem), ("grp", me_grp, n_grp)):
-        bit = 1
-        while bit < size:
-            other = me + bit * (1 - 2 * ((me // bit) % 2))
-            partners.append((me_grp, other) if name == "mem" else (other, me_mem))
-            bit *= 2
+    low = 2
+    high = n_mem // low
+    near = n_grp * low
+    me_low = lax.rem(me_mem, low)
+    me_high = me_mem // low
+    me_near = me_grp * low + me_low
+
+    def near_peer(turn):
+        other = lax.rem(me_near + turn, near)
+        return (other // low, me_high * low + lax.rem(other, low))
+
+    def far_peer(turn):
+        return (me_grp, lax.rem(me_high + turn, high) * low + me_low)
 
     barrier = pltpu.get_barrier_semaphore()
     for turn in range(1, n_mem):
         pl.semaphore_signal(
             barrier, inc=1, device_id=(me_grp, lax.rem(me_mem + turn, n_mem)), device_id_type=MESH_ID
         )
-    for partner in partners[n_mem.bit_length() - 1 :]:
-        pl.semaphore_signal(barrier, inc=1, device_id=partner, device_id_type=MESH_ID)
-    pl.semaphore_wait(barrier, n_mem - 1 + n_grp.bit_length() - 1)
+    for turn in range(1, near):
+        pl.semaphore_signal(barrier, inc=1, device_id=near_peer(turn), device_id_type=MESH_ID)
+    pl.semaphore_wait(barrier, n_mem - 1 + near - 1)
     for load in loads[:4]:
         load.wait()
 
@@ -229,23 +243,43 @@
         def _():
             z_ref[pl.ds(pl.multiple_of(me_mem * cap, cap), cap), :] = block
 
+    def exchange(value, call, size, me, peer_of, source, slots_of, sends, recvs, between=None):
+        source[call] = value
+        copies = []
+        for turn in range(1, size):
+            copies.append(
+                pltpu.make_async_remote_copy(
+                    src_ref=source.at[call],
+                    dst_ref=slots_of.at[call, me],
+                    send_sem=sends.at[call, turn - 1],
+                    recv_sem=recvs.at[call, turn - 1],
+                    device_id=peer_of(turn),
+                    device_id_type=MESH_ID,
+                )
+            )
+        for copy in copies:
+            copy.start()
+        slots_of[call, me] = value
+        if between is not None:
+            between()
+        for copy in copies:
+            copy.wait()
+        parts = [slots_of[call, i] for i in range(size)]
+        while len(parts) > 1:
+            parts = [parts[i] + parts[i + 1] for i in range(0, len(parts), 2)]
+        return parts[0]
+
     def all_sum(value, call):
-        for step, partner in enumerate(partners):
-            send[call, step] = value
-            copy = pltpu.make_async_remote_copy(
-                src_ref=send.at[call, step],
-                dst_ref=recv.at[call, step],
-                send_sem=send_sem.at[call, step],
-                recv_sem=recv_sem.at[call, step],
-                device_id=partner,
-                device_id_type=MESH_ID,
-            )
-            copy.start()
-            if step == 0:
-                for q in range(each):
-                    build(1 + call * each + q)
-            copy.wait()
-            value = value + recv[call, step]
+        def fill():
+            for q in range(each):
+                build(1 + call * each + q)
+
+        value = exchange(
+            value, call, near, me_near, near_peer, near_send, near_recv, ns_sem, nr_sem, fill
+        )
+        value = exchange(
+            value, call, high, me_high, far_peer, far_send, far_recv, fs_sem, fr_sem
+        )
         for q in range(each):
             turn = 1 + call * each + q
 
@@ -402,7 +436,7 @@
     lines = width // LANES
     slots = 2 * rows
     cap = slots // n_mem
-    steps = (n_grp.bit_length() - 1) + (n_mem.bit_length() - 1)
+    near, high = 2 * n_grp, n_mem // 2
     calls = NEWTON * (CG_ITERS + 1)
     f32, bf16, i32 = jnp.float32, jnp.bfloat16, jnp.int32
     held = pltpu.VMEM((lines, LANES), f32)
@@ -426,8 +460,10 @@
             pltpu.VMEM((1, rows), f32),
             held, held, held, held, held,
             pltpu.VMEM((1, rows), f32),
-            pltpu.VMEM((calls, steps, lines, LANES), f32),
-            pltpu.VMEM((calls, steps, lines, LANES), f32),
+            pltpu.VMEM((calls, lines, LANES), f32),
+            pltpu.VMEM((calls, near, lines, LANES), f32),
+            pltpu.VMEM((calls, lines, LANES), f32),
+            pltpu.VMEM((calls, high, lines, LANES), f32),
             pltpu.VMEM((slots, rows), bf16),
             pltpu.VMEM((n_mem - 1, cap, inner), bf16),
             pltpu.VMEM((slots, inner), bf16),
@@ -443,8 +479,10 @@
             pltpu.VMEM((8, rows), f32),
             dma((7,)),
             dma((rows // 256,)),
-            dma((calls, steps)),
-            dma((calls, steps)),
+            dma((calls, near - 1)),
+            dma((calls, near - 1)),
+            dma((calls, high - 1)),
+            dma((calls, high - 1)),
             dma((n_mem - 1,)),
             dma((n_mem - 1,)),
             dma((n_mem - 1,)),

time: 212 us -> 164 us (0.77)
  Pallas kernels: 207 us -> 159 us
    pallas_call x1, Pallas kernels: 207 us -> 159 us  [on_device(): pl.pallas_call(functools.partial(window_kernel, n_grp, n_mem), out_shape=...]
where the time goes in v3:
time: 164 us
  Pallas kernels  159 us (97%)
  local copies, waits for them, and re-layouts  3.89 us (2%)
    pallas_call x1, Pallas kernels, on_device(): pl.pallas_call(functools.partial(window_kernel, n_grp, n_mem), out_shape=...  159 us
    unnamed x3, local copies, waits for them, and re-layouts  3.89 us

profile of v3, /device:TPU:0, one launch (start us, length us, event | category | flops | bytes accessed | tf_op | source)
XLA Modules:
  0.0 163.9 jit_solution(2409829158804655477)
XLA Ops:
  0.6 159.3 %window.1 = (f32[32,128]{1,0:T(8,128)}, f32[8,256]{1,0:T(8,128)}, f32[1,1024]{1,0:T(1,128)}) custom-call(bf16[1024,4096]{1,0:T(8,128)(2,1)} %feat_hbm.1, bf16[1024,256]{1,0:T(8,128)(2,1)} %re_hbm.1, s32[1,1024]{1,0:T(1,128)} %bitcast.11, s32[1,1024]{1,0:T(1,128)} %bitcast.12, s32[1,1024]{1,0:T(1,128)} %bitcast.13, f32[1,1024]{1,0:T(1,128)} %bitcast.14, ...), custom_call_target="tpu_custom_call" | custom-call | tf_op jit(solution)/shard_map/window/pallas_call | solution.py:445
  160.0 1.3 copy.14
  161.3 1.3 copy.15
  162.6 1.3 copy.16

commit v4 on v3

--- a/solution.py
+++ b/solution.py
@@ -60,7 +60,7 @@
             value = jnp.where(sub == k, first, jnp.where(sub == k + 1, second, value))
             new.append(value)
         blocks = new
-    return blocks
+        yield blocks
 
 
 def fit_members(z_ref, zt_ref, curv_row, resid_row, local, coef_ref, gram, upper, lower):
@@ -100,48 +100,73 @@
     exact = dict(preferred_element_type=jnp.float32, precision=lax.Precision.HIGHEST)
     inverse_of = []
     heads = {}
+    rows_now = [gram[m, 0:BLOCK, :] for m in range(count)]
+    start = 0
+    later = []
+
+    def trailing(m, first, start, left_cat, right_cat):
+        update = lax.dot_general(left_cat, right_cat, TN, preferred_element_type=jnp.float32)
+        gram[m, first:width, start:width] = gram[m, first:width, start:width] - update[first - start :]
+
     for b in range(blocks):
         lo, hi = b * BLOCK, (b + 1) * BLOCK
-        squares = [gram[m, lo:hi, lo:hi] for m in range(count)]
+        squares = [rows_now[m][:, lo - start : hi - start] for m in range(count)]
         packed = [
             jnp.concatenate(squares[at : at + per], axis=1) for at in range(0, count, per)
         ]
-        packed = invert_blocks(packed)
+        for step, packed in enumerate(invert_blocks(packed)):
+            if later and step % 2 == 1:
+                later.pop(0)()
+        while later:
+            later.pop(0)()
         inverses = [
             packed[m // per][:, m % per * BLOCK : (m % per + 1) * BLOCK] for m in range(count)
         ]
         panels = []
-        if hi < width:
-            for m in range(count):
-                right = gram[m, lo:hi, hi:width]
-                panel = lax.dot_general(inverses[m], right, NN, **exact)
-                panels.append(panel)
-                a1, a2, a3 = three_parts(right)
-                b1, b2, b3 = three_parts(panel)
-                left_cat = jnp.concatenate([a1, a1, a2, a2, a1, a3], axis=0)
-                right_cat = jnp.concatenate([b1, b2, b1, b2, b3, b1], axis=0)
-                gram[m, hi:width, hi:width] = gram[m, hi:width, hi:width] - lax.dot_general(
-                    left_cat, right_cat, TN, preferred_element_type=jnp.float32
+        following = []
+        new_start = hi // LANES * LANES
+        for m in range(count):
+            head = rhs[m][:, lo - start : hi - start]
+            heads[(m, b)] = head
+            if hi == width:
+                continue
+            right = rows_now[m][:, new_start - start :]
+            panel = lax.dot_general(inverses[m], right, NN, **exact)
+            panels.append(panel)
+            a1, a2, a3 = three_parts(right)
+            b1, b2, b3 = three_parts(panel)
+            left_cat = jnp.concatenate([a1, a1, a2, a2, a1, a3], axis=0)
+            right_cat = jnp.concatenate([b1, b2, b1, b2, b3, b1], axis=0)
+            skip = hi - new_start
+            following.append(
+                gram[m, hi : hi + BLOCK, new_start:width]
+                - lax.dot_general(
+                    left_cat[:, skip : skip + BLOCK],
+                    right_cat,
+                    TN,
+                    preferred_element_type=jnp.float32,
                 )
-                now = rhs[m]
-                heads[(m, b)] = now[:, :BLOCK]
-                rhs[m] = now[:, BLOCK:] - lax.dot_general(now[:, :BLOCK], panel, NN, **exact)
-        else:
-            for m in range(count):
-                heads[(m, b)] = rhs[m]
-        inverse_of.append((inverses, panels))
-    solved = []
-    for m in range(count):
-        tail = None
-        for b in reversed(range(blocks)):
-            inverses, panels = inverse_of[b]
+            )
+            if hi + BLOCK < width:
+                later.append(
+                    functools.partial(trailing, m, hi + BLOCK, new_start, left_cat, right_cat)
+                )
+            rhs[m] = rhs[m][:, new_start - start :] - lax.dot_general(head, panel, NN, **exact)
+        rows_now = following
+        inverse_of.append((inverses, panels, new_start))
+        start = new_start
+    pieces = [[None] * blocks for _ in range(count)]
+    for b in reversed(range(blocks)):
+        inverses, panels, begin = inverse_of[b]
+        for m in range(count):
             part = lax.dot_general(heads[(m, b)], inverses[m], NN, **exact)
-            if tail is not None:
+            if panels:
+                gap = (b + 1) * BLOCK - begin
+                tail = ([jnp.zeros((1, gap), jnp.float32)] if gap else []) + pieces[m][b + 1 :]
+                tail = jnp.concatenate(tail, axis=1) if len(tail) > 1 else tail[0]
                 part = part - lax.dot_general(tail, panels[m], NT, **exact)
-                tail = jnp.concatenate([part, tail], axis=1)
-            else:
-                tail = part
-        solved.append(tail)
+            pieces[m][b] = part
+    solved = [jnp.concatenate(pieces[m], axis=1) for m in range(count)]
     coef = -jnp.concatenate(solved, axis=0)
     coef_ref[...] = coef
     high = coef.astype(jnp.bfloat16)

time: 164 us -> 157 us (0.957)
  Pallas kernels: 159 us -> 152 us
    pallas_call x1, Pallas kernels: 159 us -> 152 us  [on_device(): pl.pallas_call(functools.partial(window_kernel, n_grp, n_mem), out_shape=...]
where the time goes in v4:
time: 157 us; the launch traced here: 156 us
  Pallas kernels  152 us (97%)
  local copies, waits for them, and re-layouts  3.89 us (2%)
    pallas_call x1, Pallas kernels, on_device(): pl.pallas_call(functools.partial(window_kernel, n_grp, n_mem), out_shape=...  152 us
    unnamed x3, local copies, waits for them, and re-layouts  3.89 us

profile of v4, /device:TPU:0, one launch (start us, length us, event | category | flops | bytes accessed | tf_op | source)
XLA Modules:
  0.0 156.2 jit_solution(8666760617349105828)
XLA Ops:
  0.6 151.7 %window.1 = (f32[32,128]{1,0:T(8,128)}, f32[8,256]{1,0:T(8,128)}, f32[1,1024]{1,0:T(1,128)}) custom-call(bf16[1024,4096]{1,0:T(8,128)(2,1)} %feat_hbm.1, bf16[1024,256]{1,0:T(8,128)(2,1)} %re_hbm.1, s32[1,1024]{1,0:T(1,128)} %bitcast.11, s32[1,1024]{1,0:T(1,128)} %bitcast.12, s32[1,1024]{1,0:T(1,128)} %bitcast.13, f32[1,1024]{1,0:T(1,128)} %bitcast.14, ...), custom_call_target="tpu_custom_call" | custom-call | tf_op jit(solution)/shard_map/window/pallas_call | solution.py:470
  152.3 1.3 copy.14
  153.7 1.3 copy.15
  155.0 1.3 copy.16
